TPU v7x, 512 devices: a whole 4x4x16 slice. The times are simulated.
512 devices in a mesh: ctx: 32 (over y, x, z_hi), head: 16 (over z_lo, core).
Axes of the slice: x: 4, y: 4, z: 16 (z_hi: 2, z_lo: 8; z = z_hi * 8 + z_lo), core: 2. Of those that a mesh axis runs over, the one named last changes fastest.
Arguments:
- tokens: bfloat16 [14336, 5376], P('ctx'), may hold values from -6 to 6
- w_query: bfloat16 [5376, 4096], P('ctx', 'head')
- key_weight: bfloat16 [5376, 2048], P('ctx', 'head')
- value_weight: bfloat16 [5376, 2048], P('ctx', 'head'), may hold values from -0.078125 to 0.078125
- query_gain: float32 [128], replicated, may hold values from 0.5 to 16
- key_gain: float32 [128], replicated, may hold values from 0.5 to 16
Outputs:
- attended: bfloat16 [14336, 4096], P('ctx', 'head')
All inputs are finite; a program needn't handle non-finite values.
Results may differ from a plain program's by a relative error of at most 0.025.
Values may be sent and summed in bfloat16 or wider, within the bound.
No kernel may reach another device: no remote copies, remote signals or barrier semaphores. Data moves between devices by JAX's collectives and lax.ppermute only.
A program may use at most 64 MiB of HBM per device.

v0:
```python
import jax
import jax.numpy as jnp
from jax import lax
from jax.sharding import Mesh
from jax.sharding import PartitionSpec as P

WINDOW = 1024
PLANE = ("y", "x")
CTX = ("y", "x", "zh")
HEAD = ("zl", "core")
query_scale = 168.0 ** (-0.5)


def normalize(values, gain):
    return values * lax.rsqrt(jnp.mean(values * values, axis=-1, keepdims=True) + 1e-06) * gain


def rotate(values, position):
    half = values.shape[-1] // 2
    expo = jnp.arange(half, dtype=jnp.float32) * (2.0 / values.shape[-1])
    freq = jnp.power(jnp.float32(10000.0), -expo)
    angle = position[:, None] * freq[None, :]
    cosine = jnp.cos(angle)[:, None, :]
    sine = jnp.sin(angle)[:, None, :]
    first = values[..., :half]
    second = values[..., half:]
    return jnp.concatenate(
        [first * cosine - second * sine, second * cosine + first * sine], axis=-1
    )


def from_behind(block, distance):
    count = lax.axis_size(CTX)
    return lax.ppermute(block, CTX, [(i - distance, i) for i in range(distance, count)])


def on_device(tokens, w_query, key_weight, value_weight, query_gain, key_gain):
    row_count = tokens.shape[0]
    head_size = query_gain.shape[0]
    plane = lax.axis_size(PLANE)
    q_width = w_query.shape[1]
    kv_width = 2 * head_size
    mine = jnp.concatenate([key_weight, value_weight, w_query], axis=1)
    pair = lax.all_gather(mine, "zh", axis=0, tiled=True)
    pair_kv = pair[:, :kv_width]
    pair_q = pair[:, kv_width:]
    all_q = lax.all_gather(pair_q, PLANE, axis=0, tiled=True)
    all_kv = lax.all_to_all(
        jnp.broadcast_to(pair_kv[None], (plane,) + pair_kv.shape), PLANE, 0, 0, tiled=True
    ).reshape(-1, kv_width)
    offset = lax.axis_index(CTX) * row_count
    local_pos = offset + jnp.arange(row_count, dtype=jnp.int32)
    position = local_pos.astype(jnp.float32)
    kv_sum = jnp.dot(tokens, all_kv, preferred_element_type=jnp.float32)
    keys = rotate(normalize(kv_sum[:, None, :head_size], key_gain), position)[:, 0]
    kv = jnp.concatenate(
        [keys.astype(jnp.bfloat16), kv_sum[:, head_size:].astype(jnp.bfloat16)], axis=1
    )
    reach = WINDOW - 1
    hop_count = (reach + row_count - 1) // row_count
    needed = [min(row_count, reach - distance * row_count) for distance in range(hop_count)]
    sizes = [-(-rows // 16) * 16 for rows in needed]
    received = [
        from_behind(kv[row_count - size :], distance + 1) for distance, size in enumerate(sizes)
    ]
    before = sum(sizes)
    all_keys_values = jnp.concatenate(received[::-1] + [kv], axis=0)
    key_pos = offset - before + jnp.arange(before + row_count, dtype=jnp.int32)
    query_sum = jnp.dot(tokens, all_q, preferred_element_type=jnp.float32)
    queries = rotate(
        normalize(query_sum.reshape(row_count, 2, head_size), query_gain), position
    ).astype(jnp.bfloat16)
    allowed = (
        (key_pos[None, :] <= local_pos[:, None])
        & (key_pos[None, :] > local_pos[:, None] - WINDOW)
        & (key_pos[None, :] >= 0)
    )
    scores = (
        jnp.einsum(
            "bgd,cd->gbc",
            queries,
            all_keys_values[:, :head_size],
            preferred_element_type=jnp.float32,
        )
        * query_scale
    )
    scores = jnp.where(allowed[None], scores, jnp.float32(-1e30))
    top = jnp.max(scores, axis=-1, keepdims=True)
    weights = jnp.exp(scores - top)
    probs = (weights / jnp.sum(weights, axis=-1, keepdims=True)).astype(jnp.bfloat16)
    mixed = jnp.einsum(
        "gbc,cd->bgd", probs, all_keys_values[:, head_size:], preferred_element_type=jnp.float32
    )
    return mixed.reshape(row_count, q_width).astype(jnp.bfloat16)


def solution(mesh):
    split = Mesh(mesh.devices.reshape(4, 4, 2, 8, 2), CTX + HEAD)
    placed = (P(CTX, None), P(CTX, HEAD), P(CTX, HEAD), P(CTX, HEAD), P(), P())
    return jax.shard_map(
        on_device, mesh=split, in_specs=placed, out_specs=P(CTX, HEAD), check_vma=False
    )
```

profile of v0, /device:TPU:50, one launch (start us, length us, event | category | flops | bytes accessed | tf_op | source)
XLA Modules:
  0.0 148.6 jit_solution(11865930825600269100)
XLA Ops:
  6.5 0.9 pad_maximum_fusion.2
  7.5 27.9 %all_gather.6 = bf16[336,512]{1,0:T(8,128)(2,1)S(1)} all-gather(bf16[168,512]{1,0:T(8,128)(2,1)S(1)} %pad_maximum_fusion.2), channel_id=1, replica_groups=mesh['y'=4,'x'=4,'zh'=2,'zl'=8,'core'=2] {'zh'}, dimensions={0}, use_global_device_ids=true | all-gather | bytes 516096 | tf_op jit(solution)/shard_map/all_gather | solution.py:44
  35.4 0.7 fusion.30
  36.1 0.0 all-gather.2.cloned.1.call-update
  36.1 1.7 %broadcast_in_dim.10 = bf16[16,336,256]{2,1,0:T(8,128)(2,1)} broadcast(bf16[336,256]{1,0:T(8,128)(2,1)S(1)} %get-tuple-element.8), dimensions={1,2} | broadcast | bytes 2924544 | tf_op jit(solution)/shard_map/broadcast_in_dim | solution.py:49
  37.8 7.3 %all-to-all-start = ((bf16[16,336,256]{2,1,0:T(8,128)(2,1)}), bf16[16,336,256]{2,1,0:T(8,128)(2,1)S(1)}, u32[]{:S(2)}, u32[]{:S(2)}) async-start(bf16[16,336,256]{2,1,0:T(8,128)(2,1)} %broadcast_in_dim.10), calls=%async_computation | async-start | bytes 5505024 | tf_op jit(solution)/shard_map/all_to_all | solution.py:48
  45.1 0.7 and_and_fusion
  45.8 36.0 %all-to-all-done = bf16[16,336,256]{2,1,0:T(8,128)(2,1)S(1)} async-done(((bf16[16,336,256]{2,1,0:T(8,128)(2,1)}), bf16[16,336,256]{2,1,0:T(8,128)(2,1)S(1)}, u32[]{:S(2)}, u32[]{:S(2)}) %all-to-all-start) | async-done | bytes 2752544 | tf_op jit(solution)/shard_map/all_to_all | solution.py:48
  81.8 3.8 %convolution_bitcast_fusion = f32[448,256]{1,0:T(8,128)S(1)} fusion(bf16[448,5376]{1,0:T(8,128)(2,1)} %param.6, bf16[5376,256]{1,0:T(8,128)(2,1)S(1)} %bitcast.52), kind=kOutput, calls=%fused_computation.10 | convolution fusion | flops 1233125376 | bytes 8028160 | tf_op jit(solution)/shard_map/dot_general | solution.py:54
  85.7 0.1 multiply_reduce_fusion.1
  85.8 0.1 multiply_bitcast_fusion
  86.0 1.1 fusion.17
  87.1 0.1 maximum_bitcast_fusion
  87.2 3.3 %collective-permute-start.1 = (bf16[448,256]{1,0:T(8,128)(2,1)S(1)}, bf16[448,256]{1,0:T(8,128)(2,1)S(1)}, u32[]{:S(2)}, u32[]{:S(2)}) collective-permute-start(bf16[448,256]{1,0:T(8,128)(2,1)S(1)} %pad_maximum_fusion), channel_id=1, source_target_pairs={{0,32},{16,48},{32,64},{48,80},{64,96},{80,112},{96,128},{112,144}... | collective-permute-start | bytes 688136 | tf_op jit(solution)/shard_map/ppermute | solution.py:34
  90.5 12.5 %collective-permute-start.2 = (bf16[448,256]{1,0:T(8,128)(2,1)S(1)}, bf16[448,256]{1,0:T(8,128)(2,1)S(1)}, u32[]{:S(2)}, u32[]{:S(2)}) collective-permute-start(bf16[448,256]{1,0:T(8,128)(2,1)S(1)} %pad_maximum_fusion), channel_id=1, source_target_pairs={{0,16},{16,32},{32,48},{48,64},{64,80},{80,96},{96,112},{112,128},... | collective-permute-start | bytes 688136 | tf_op jit(solution)/shard_map/ppermute | solution.py:34
  103.1 7.0 %collective-permute-start = (bf16[128,256]{1,0:T(8,128)(2,1)S(1)}, bf16[128,256]{1,0:T(8,128)(2,1)S(1)}, u32[]{:S(2)}, u32[]{:S(2)}) collective-permute-start(bf16[128,256]{1,0:T(8,128)(2,1)S(1)} %fusion.20), channel_id=1, source_target_pairs={{0,48},{16,64},{32,80},{48,96},{64,112},{80,128},{96,144},{112,160... | collective-permute-start | bytes 196616 | tf_op jit(solution)/shard_map/ppermute | solution.py:34
  110.1 0.9 multiply_cosine_fusion
  111.0 17.8 %collective-permute-done = bf16[128,256]{1,0:T(8,128)(2,1)S(1)} collective-permute-done((bf16[128,256]{1,0:T(8,128)(2,1)S(1)}, bf16[128,256]{1,0:T(8,128)(2,1)S(1)}, u32[]{:S(2)}, u32[]{:S(2)}) %collective-permute-start) | collective-permute-done | bytes 65568 | tf_op jit(solution)/shard_map/ppermute | solution.py:34
  128.8 0.0 collective-permute-done.2
  128.8 0.1 maximum_maximum_fusion
  128.9 0.0 copy-start
  128.9 0.0 all-gather.2.cloned.1.call-done
  128.9 4.7 %fusion.32 = f32[256,448]{0,1:T(8,128)S(1)} fusion(bf16[448,5376]{1,0:T(8,128)(2,1)} %param.6, bf16[5376,256]{1,0:T(8,128)(2,1)} %all-gather.2.cloned.1.call-done), kind=kOutput, calls=%fused_computation.61 | convolution fusion | flops 1233125376 | bytes 8028160 | tf_op jit(solution)/shard_map/dot_general | solution.py:69
  133.6 0.2 reshape.229
  133.8 0.5 multiply_reduce_fusion
  134.4 0.1 copy.13
  134.5 0.0 copy-done
  134.5 0.2 fusion.10
  134.7 0.2 subtract_convert_fusion
  134.9 2.3 %fusion.31 = f32[2,448]{1,0:T(2,128)S(1)} fusion(pred[448,1472]{1,0:T(8,128)(4,1)S(1)} %and_and_fusion, bf16[1472,256]{1,0:T(8,128)(2,1)S(1)} %maximum_maximum_fusion, bf16[448,2,64]{2,0,1:T(8,128)(2,1)S(1)} %get-tuple-element.6, bf16[448,2,64]{2,0,1:T(8,128)(2,1)S(1)} %get-tuple-element.5), kind=kOutput, calls=%fused_computation.60 | convolution fusion | flops 343377344 | bytes 1527296 | tf_op jit(solution)/shard_map/sub | solution.py:89
  137.2 3.8 %fusion.7 = bf16[2,56,8,128]{3,2,1,0:T(8,128)(2,1)S(1)} fusion(f32[2,448]{1,0:T(2,128)S(1)} %fusion.31, bf16[1472,256]{1,0:T(8,128)(2,1)S(1)} %maximum_maximum_fusion, pred[448,1472]{1,0:T(8,128)(4,1)S(1)} %and_and_fusion, bf16[448,2,64]{2,0,1:T(8,128)(2,1)S(1)} %get-tuple-element.6, bf16[448,2,64]{2,0,1:T(8,128)(2,1)S(1)} %get-tuple-element.5), kind=kOutput, calls=%fused_computation.12 | convolution fusion | flops 682453312 | bytes 1875456 | tf_op jit(solution)/shard_map/gbc,cd->bgd/dot_general | solution.py:91
  141.0 0.7 copy.20
  (14 shorter events, 0.1 us)
Async XLA Ops:
  6.5 122.4 %all-gather.2.cloned.1.call-start = ((), (), s32[]{:S(2)}) async-start(), calls=%async_computation.1 | async-start | bytes 2924544 | tf_op jit(solution)/shard_map/all_gather | solution.py:47
  37.8 44.0 %all-to-all-start = ((bf16[16,336,256]{2,1,0:T(8,128)(2,1)}), bf16[16,336,256]{2,1,0:T(8,128)(2,1)S(1)}, u32[]{:S(2)}, u32[]{:S(2)}) async-start(bf16[16,336,256]{2,1,0:T(8,128)(2,1)} %broadcast_in_dim.10), calls=%async_computation | async-start | bytes 5505024 | tf_op jit(solution)/shard_map/all_to_all | solution.py:48
  81.8 4.0 %copy-start.1 = (f32[128]{0:T(128)S(1)}, f32[128]{0:T(128)}, u32[]{:S(2)}) copy-start(f32[128]{0:T(128)} %param.11) | copy-start | bytes 1540
  87.2 41.6 %collective-permute-start.1 = (bf16[448,256]{1,0:T(8,128)(2,1)S(1)}, bf16[448,256]{1,0:T(8,128)(2,1)S(1)}, u32[]{:S(2)}, u32[]{:S(2)}) collective-permute-start(bf16[448,256]{1,0:T(8,128)(2,1)S(1)} %pad_maximum_fusion), channel_id=1, source_target_pairs={{0,32},{16,48},{32,64},{48,80},{64,96},{80,112},{96,128},{112,144}... | collective-permute-start | bytes 688136 | tf_op jit(solution)/shard_map/ppermute | solution.py:34
  90.5 38.3 %collective-permute-start.2 = (bf16[448,256]{1,0:T(8,128)(2,1)S(1)}, bf16[448,256]{1,0:T(8,128)(2,1)S(1)}, u32[]{:S(2)}, u32[]{:S(2)}) collective-permute-start(bf16[448,256]{1,0:T(8,128)(2,1)S(1)} %pad_maximum_fusion), channel_id=1, source_target_pairs={{0,16},{16,32},{32,48},{48,64},{64,80},{80,96},{96,112},{112,128},... | collective-permute-start | bytes 688136 | tf_op jit(solution)/shard_map/ppermute | solution.py:34
  103.1 25.7 %collective-permute-start = (bf16[128,256]{1,0:T(8,128)(2,1)S(1)}, bf16[128,256]{1,0:T(8,128)(2,1)S(1)}, u32[]{:S(2)}, u32[]{:S(2)}) collective-permute-start(bf16[128,256]{1,0:T(8,128)(2,1)S(1)} %fusion.20), channel_id=1, source_target_pairs={{0,48},{16,64},{32,80},{48,96},{64,112},{80,128},{96,144},{112,160... | collective-permute-start | bytes 196616 | tf_op jit(solution)/shard_map/ppermute | solution.py:34
  128.9 5.6 %copy-start = (f32[128]{0:T(128)S(1)}, f32[128]{0:T(128)}, u32[]{:S(2)}) copy-start(f32[128]{0:T(128)} %param.10) | copy-start | bytes 1540
Sparse Core Ops, SparseCore 0:
  36.2 82.0 all-gather.1
where the time goes:
time: 149 us
  waiting for transfers between devices  53.9 us (36%)
  starting transfers between devices  30.1 us (20%)
  blocking collectives  27.9 us (19%)
  matrix products  14.5 us (10%)
  between operations  13.6 us (9%)
  other arithmetic  5.06 us (3%)
  local copies, waits for them, and re-layouts  3.53 us (2%)
    all_to_all x1, waiting for transfers between devices, on_device(): lax.all_to_all(jnp.broadcast_to(pair_kv[None], (plane,) + pair_kv.shape),...  36 us
    all_gather x1, blocking collectives, on_device(): pair = lax.all_gather(mine, 'zh', axis=0, tiled=True)  27.9 us
    ppermute x3, starting transfers between devices, from_behind(): lax.ppermute(block, CTX, [(i - distance, i) for i in range(distance, coun...  22.8 us
    ppermute x3, waiting for transfers between devices, from_behind(): lax.ppermute(block, CTX, [(i - distance, i) for i in range(distance, coun...  17.8 us
    all_to_all x1, starting transfers between devices, on_device(): lax.all_to_all(jnp.broadcast_to(pair_kv[None], (plane,) + pair_kv.shape),...  7.25 us
    dot_general x1, matrix products, on_device(): query_sum = jnp.dot(tokens, all_q, preferred_element_type=jnp.float32)  4.65 us
    dot_general x1, matrix products, on_device(): kv_sum = jnp.dot(tokens, all_kv, preferred_element_type=jnp.float32)  3.78 us
    dot_general x1, matrix products, on_device(): jnp.einsum('gbc,cd->bgd', probs, all_keys_values[:, head_size:], preferre...  3.76 us
  transfers between devices with their start and end apart: 5, of which 2 were waited for; matrix products, arithmetic and copies ran while one was open for 6% of the time, Pallas kernels for 0%

commit v1 on v0

--- a/solution.py
+++ b/solution.py
@@ -9,6 +9,16 @@
 CTX = ("y", "x", "zh")
 HEAD = ("zl", "core")
 query_scale = 168.0 ** (-0.5)
+
+
+def store_desk(x_local, in_dim):
+    upper = jnp.concatenate(
+        lax.all_to_all(
+            jnp.stack([x_local for _ in range(lax.axis_size("zh"))], axis=0), "zh", 0, 0
+        ),
+        axis=in_dim,
+    )
+    return upper
 
 
 def normalize(values, gain):
@@ -41,7 +51,7 @@
     q_width = w_query.shape[1]
     kv_width = 2 * head_size
     mine = jnp.concatenate([key_weight, value_weight, w_query], axis=1)
-    pair = lax.all_gather(mine, "zh", axis=0, tiled=True)
+    pair = store_desk(mine, 0)
     pair_kv = pair[:, :kv_width]
     pair_q = pair[:, kv_width:]
     all_q = lax.all_gather(pair_q, PLANE, axis=0, tiled=True)

time: 149 us -> 156 us (1.047)
  the two profiles are of different devices: /device:TPU:50 before, /device:TPU:40 now
where the time goes in v1:
time: 156 us
  waiting for transfers between devices  55.7 us (36%)
  blocking collectives  39.8 us (26%)
  starting transfers between devices  23.6 us (15%)
  matrix products  14.5 us (9%)
  between operations  13.6 us (9%)
  other arithmetic  5.09 us (3%)
  local copies, waits for them, and re-layouts  3.53 us (2%)
    all_to_all x1, blocking collectives, store_desk(): lax.all_to_all(jnp.stack([x_local for _ in range(lax.axis_size('zh'))], a...  39.8 us
    all_to_all x1, waiting for transfers between devices, on_device(): lax.all_to_all(jnp.broadcast_to(pair_kv[None], (plane,) + pair_kv.shape),...  39.8 us
    ppermute x3, starting transfers between devices, from_behind(): lax.ppermute(block, CTX, [(i - distance, i) for i in range(distance, coun...  16.2 us
    ppermute x3, waiting for transfers between devices, from_behind(): lax.ppermute(block, CTX, [(i - distance, i) for i in range(distance, coun...  15.9 us
    all_to_all x1, starting transfers between devices, on_device(): lax.all_to_all(jnp.broadcast_to(pair_kv[None], (plane,) + pair_kv.shape),...  7.39 us
    dot_general x1, matrix products, on_device(): query_sum = jnp.dot(tokens, all_q, preferred_element_type=jnp.float32)  4.65 us
    dot_general x1, matrix products, on_device(): kv_sum = jnp.dot(tokens, all_kv, preferred_element_type=jnp.float32)  3.78 us
    dot_general x1, matrix products, on_device(): jnp.einsum('gbc,cd->bgd', probs, all_keys_values[:, head_size:], preferre...  3.76 us
  transfers between devices with their start and end apart: 5, of which 2 were waited for; matrix products, arithmetic and copies ran while one was open for 6% of the time, Pallas kernels for 0%

profile of v1, /device:TPU:40, one launch (start us, length us, event | category | flops | bytes accessed | tf_op | source)
XLA Modules:
  0.0 155.8 jit_solution(15544655499507934611)
XLA Ops:
  6.5 0.9 maximum_bitcast_fusion
  7.5 39.8 %all_to_all.10 = bf16[2,168,512]{2,1,0:T(8,128)(2,1)S(1)} all-to-all(bf16[2,168,512]{2,1,0:T(8,128)(2,1)S(1)} %pad_maximum_fusion), channel_id=1, replica_groups=mesh['y'=4,'x'=4,'zh'=2,'zl'=8,'core'=2] {'zh'}, dimensions={0} | all-to-all | bytes 688128 | tf_op jit(solution)/shard_map/all_to_all | solution.py:16
  47.3 0.7 fusion.30
  48.0 0.0 all-gather.2.cloned.1.call-update
  48.0 1.7 %broadcast_in_dim.10 = bf16[16,336,256]{2,1,0:T(8,128)(2,1)} broadcast(bf16[336,256]{1,0:T(8,128)(2,1)S(1)} %get-tuple-element.8), dimensions={1,2} | broadcast | bytes 2924544 | tf_op jit(solution)/shard_map/broadcast_in_dim | solution.py:59
  49.8 7.4 %all-to-all-start.1 = ((bf16[16,336,256]{2,1,0:T(8,128)(2,1)}), bf16[16,336,256]{2,1,0:T(8,128)(2,1)S(1)}, u32[]{:S(2)}, u32[]{:S(2)}) async-start(bf16[16,336,256]{2,1,0:T(8,128)(2,1)} %broadcast_in_dim.10), calls=%async_computation.1 | async-start | bytes 5505024 | tf_op jit(solution)/shard_map/all_to_all | solution.py:58
  57.2 0.7 and_and_fusion
  57.9 39.8 %all-to-all-done.1 = bf16[16,336,256]{2,1,0:T(8,128)(2,1)S(1)} async-done(((bf16[16,336,256]{2,1,0:T(8,128)(2,1)}), bf16[16,336,256]{2,1,0:T(8,128)(2,1)S(1)}, u32[]{:S(2)}, u32[]{:S(2)}) %all-to-all-start.1) | async-done | bytes 2752544 | tf_op jit(solution)/shard_map/all_to_all | solution.py:58
  97.7 3.8 %convolution_bitcast_fusion = f32[448,256]{1,0:T(8,128)S(1)} fusion(bf16[448,5376]{1,0:T(8,128)(2,1)} %param.6, bf16[5376,256]{1,0:T(8,128)(2,1)S(1)} %bitcast.55), kind=kOutput, calls=%fused_computation.10 | convolution fusion | flops 1233125376 | bytes 8028160 | tf_op jit(solution)/shard_map/dot_general | solution.py:64
  101.5 0.1 multiply_reduce_fusion.1
  101.7 0.1 multiply_bitcast_fusion
  101.8 1.1 fusion.17
  102.9 0.1 maximum_bitcast_fusion.1
  103.1 1.9 %collective-permute-start.1 = (bf16[448,256]{1,0:T(8,128)(2,1)S(1)}, bf16[448,256]{1,0:T(8,128)(2,1)S(1)}, u32[]{:S(2)}, u32[]{:S(2)}) collective-permute-start(bf16[448,256]{1,0:T(8,128)(2,1)S(1)} %pad_maximum_fusion.1), channel_id=1, source_target_pairs={{0,32},{16,48},{32,64},{48,80},{64,96},{80,112},{96,128},{112,144}... | collective-permute-start | bytes 688136 | tf_op jit(solution)/shard_map/ppermute | solution.py:44
  105.0 1.9 %collective-permute-start.2 = (bf16[448,256]{1,0:T(8,128)(2,1)S(1)}, bf16[448,256]{1,0:T(8,128)(2,1)S(1)}, u32[]{:S(2)}, u32[]{:S(2)}) collective-permute-start(bf16[448,256]{1,0:T(8,128)(2,1)S(1)} %pad_maximum_fusion.1), channel_id=1, source_target_pairs={{0,16},{16,32},{32,48},{48,64},{64,80},{80,96},{96,112},{112,128},... | collective-permute-start | bytes 688136 | tf_op jit(solution)/shard_map/ppermute | solution.py:44
  106.9 12.3 %collective-permute-start = (bf16[128,256]{1,0:T(8,128)(2,1)S(1)}, bf16[128,256]{1,0:T(8,128)(2,1)S(1)}, u32[]{:S(2)}, u32[]{:S(2)}) collective-permute-start(bf16[128,256]{1,0:T(8,128)(2,1)S(1)} %fusion.20), channel_id=1, source_target_pairs={{0,48},{16,64},{32,80},{48,96},{64,112},{80,128},{96,144},{112,160... | collective-permute-start | bytes 196616 | tf_op jit(solution)/shard_map/ppermute | solution.py:44
  119.3 0.9 multiply_cosine_fusion
  120.1 15.9 %collective-permute-done = bf16[128,256]{1,0:T(8,128)(2,1)S(1)} collective-permute-done((bf16[128,256]{1,0:T(8,128)(2,1)S(1)}, bf16[128,256]{1,0:T(8,128)(2,1)S(1)}, u32[]{:S(2)}, u32[]{:S(2)}) %collective-permute-start) | collective-permute-done | bytes 65568 | tf_op jit(solution)/shard_map/ppermute | solution.py:44
  136.0 0.0 collective-permute-done.1
  136.0 0.1 maximum_maximum_fusion
  136.1 0.0 copy-start
  136.1 0.0 all-gather.2.cloned.1.call-done
  136.1 4.7 %fusion.32 = f32[256,448]{0,1:T(8,128)S(1)} fusion(bf16[448,5376]{1,0:T(8,128)(2,1)} %param.6, bf16[5376,256]{1,0:T(8,128)(2,1)} %all-gather.2.cloned.1.call-done), kind=kOutput, calls=%fused_computation.62 | convolution fusion | flops 1233125376 | bytes 8028160 | tf_op jit(solution)/shard_map/dot_general | solution.py:79
  140.8 0.2 reshape.233
  141.0 0.5 multiply_reduce_fusion
  141.6 0.1 copy.13
  141.7 0.0 copy-done
  141.7 0.2 fusion.10
  141.9 0.2 subtract_convert_fusion
  142.1 2.3 %fusion.31 = f32[2,448]{1,0:T(2,128)S(1)} fusion(pred[448,1472]{1,0:T(8,128)(4,1)S(1)} %and_and_fusion, bf16[1472,256]{1,0:T(8,128)(2,1)S(1)} %maximum_maximum_fusion, bf16[448,2,64]{2,0,1:T(8,128)(2,1)S(1)} %get-tuple-element.6, bf16[448,2,64]{2,0,1:T(8,128)(2,1)S(1)} %get-tuple-element.5), kind=kOutput, calls=%fused_computation.61 | convolution fusion | flops 343377344 | bytes 1527296 | tf_op jit(solution)/shard_map/sub | solution.py:99
  144.4 3.8 %fusion.7 = bf16[2,56,8,128]{3,2,1,0:T(8,128)(2,1)S(1)} fusion(f32[2,448]{1,0:T(2,128)S(1)} %fusion.31, bf16[1472,256]{1,0:T(8,128)(2,1)S(1)} %maximum_maximum_fusion, pred[448,1472]{1,0:T(8,128)(4,1)S(1)} %and_and_fusion, bf16[448,2,64]{2,0,1:T(8,128)(2,1)S(1)} %get-tuple-element.6, bf16[448,2,64]{2,0,1:T(8,128)(2,1)S(1)} %get-tuple-element.5), kind=kOutput, calls=%fused_computation.12 | convolution fusion | flops 682453312 | bytes 1875456 | tf_op jit(solution)/shard_map/gbc,cd->bgd/dot_general | solution.py:101
  148.2 0.7 copy.20
  (15 shorter events, 0.1 us)
Async XLA Ops:
  6.5 129.6 %all-gather.2.cloned.1.call-start = ((), (), s32[]{:S(2)}) async-start(), calls=%async_computation.2 | async-start | bytes 2924544 | tf_op jit(solution)/shard_map/all_gather | solution.py:57
  49.8 47.9 %all-to-all-start.1 = ((bf16[16,336,256]{2,1,0:T(8,128)(2,1)}), bf16[16,336,256]{2,1,0:T(8,128)(2,1)S(1)}, u32[]{:S(2)}, u32[]{:S(2)}) async-start(bf16[16,336,256]{2,1,0:T(8,128)(2,1)} %broadcast_in_dim.10), calls=%async_computation.1 | async-start | bytes 5505024 | tf_op jit(solution)/shard_map/all_to_all | solution.py:58
  97.7 4.0 %copy-start.1 = (f32[128]{0:T(128)S(1)}, f32[128]{0:T(128)}, u32[]{:S(2)}) copy-start(f32[128]{0:T(128)} %param.11) | copy-start | bytes 1540
  103.1 33.0 %collective-permute-start.1 = (bf16[448,256]{1,0:T(8,128)(2,1)S(1)}, bf16[448,256]{1,0:T(8,128)(2,1)S(1)}, u32[]{:S(2)}, u32[]{:S(2)}) collective-permute-start(bf16[448,256]{1,0:T(8,128)(2,1)S(1)} %pad_maximum_fusion.1), channel_id=1, source_target_pairs={{0,32},{16,48},{32,64},{48,80},{64,96},{80,112},{96,128},{112,144}... | collective-permute-start | bytes 688136 | tf_op jit(solution)/shard_map/ppermute | solution.py:44
  105.0 31.0 %collective-permute-start.2 = (bf16[448,256]{1,0:T(8,128)(2,1)S(1)}, bf16[448,256]{1,0:T(8,128)(2,1)S(1)}, u32[]{:S(2)}, u32[]{:S(2)}) collective-permute-start(bf16[448,256]{1,0:T(8,128)(2,1)S(1)} %pad_maximum_fusion.1), channel_id=1, source_target_pairs={{0,16},{16,32},{32,48},{48,64},{64,80},{80,96},{96,112},{112,128},... | collective-permute-start | bytes 688136 | tf_op jit(solution)/shard_map/ppermute | solution.py:44
  106.9 29.1 %collective-permute-start = (bf16[128,256]{1,0:T(8,128)(2,1)S(1)}, bf16[128,256]{1,0:T(8,128)(2,1)S(1)}, u32[]{:S(2)}, u32[]{:S(2)}) collective-permute-start(bf16[128,256]{1,0:T(8,128)(2,1)S(1)} %fusion.20), channel_id=1, source_target_pairs={{0,48},{16,64},{32,80},{48,96},{64,112},{80,128},{96,144},{112,160... | collective-permute-start | bytes 196616 | tf_op jit(solution)/shard_map/ppermute | solution.py:44
  136.1 5.6 %copy-start = (f32[128]{0:T(128)S(1)}, f32[128]{0:T(128)}, u32[]{:S(2)}) copy-start(f32[128]{0:T(128)} %param.10) | copy-start | bytes 1540
Sparse Core Ops, SparseCore 0:
  48.1 73.3 all-gather.1
